TPU v7x, 32 devices: a whole 2x2x4 slice. The times are simulated.
32 devices in a mesh: dp: 8 (over z, core), space: 4 (over y, x).
Axes of the slice: x: 2, y: 2, z: 4, core: 2. Of those that a mesh axis runs over, the one named last changes fastest.
Arguments:
- inputs: bfloat16 [8, 24, 32, 32, 256], P('dp', 'space'), may hold values from -6 to 6
- kernels: bfloat16 [2, 3, 3, 256, 256], P(None, None, None, 'dp'), may hold values from -0.125 to 0.125
- cotangent: bfloat16 [8, 24, 32, 32, 256], P('dp', 'space'), may hold values from -0.01171875 to 0.01171875
- adjacency: int32 [24, 4, 3], P('space'), may hold values from 0 to 23, as said below
Outputs:
- final_state: bfloat16 [8, 24, 32, 32, 256], P('dp', 'space')
- kernel_grads: float32 [2, 3, 3, 256, 256], P(None, None, None, 'dp')
Inputs may be any that keep to these rules, and one draw needn't show every extreme that they name: Entry [t, e] = (n, f, r): edge e of tile t meets edge f of tile n, and r = 1 where the two edges are read in opposite directions along the shared line. The relation is symmetric: adjacency[n, f] = (t, e, r). The tiles form 2 x 2 blocks on the six faces of a cube, numbered in an order drawn from the seed.
All inputs are finite; a program needn't handle non-finite values.
Results may differ from a plain program's by a relative error of at most 0.005.
Values may be sent and summed in bfloat16 or wider, within the bound.
A program may use at most 192 MiB of HBM per device.

v0:
```python
import jax
import jax.numpy as jnp
from jax import lax
from jax.sharding import PartitionSpec as P

LAYERS = 2


def edge_strips(tile_field):
    return jnp.stack(
        [
            tile_field[:, :, 0],
            tile_field[:, :, -1],
            tile_field[:, :, :, 0],
            tile_field[:, :, :, -1],
        ],
        axis=2,
    )


def orient(strips, adjacency):
    selected = strips[:, adjacency[:, :, 0], adjacency[:, :, 1]]
    flipped = (adjacency[:, :, 2] == 1)[None, :, :, None, None]
    return jnp.where(flipped, selected[:, :, :, ::-1], selected)


def neighbor_rims(tile_field, adjacency):
    gathered = lax.all_gather(edge_strips(tile_field), "space", axis=1, tiled=True)
    return orient(gathered, adjacency)


def returned_rims(rim_values, adjacency):
    gathered = lax.all_gather(rim_values, "space", axis=1, tiled=True)
    return orient(gathered, adjacency)


def with_rim(tile_field, rim_rows):
    middle = jnp.concatenate(
        [rim_rows[:, :, 2][:, :, :, None], tile_field, rim_rows[:, :, 3][:, :, :, None]], axis=3
    )
    corner = jnp.zeros(tile_field.shape[:2] + (1, tile_field.shape[4]), tile_field.dtype)
    top_row = jnp.concatenate([corner, rim_rows[:, :, 0], corner], axis=2)[:, :, None]
    bottom_row = jnp.concatenate([corner, rim_rows[:, :, 1], corner], axis=2)[:, :, None]
    return jnp.concatenate([top_row, middle, bottom_row], axis=2)


def convolve(padded, kernel):
    extent = padded.shape[2] - 2
    channels = padded.shape[-1]
    summed = jnp.zeros(padded.shape[:2] + (extent, extent, kernel.shape[-1]), jnp.float32)
    for row_off in range(3):
        for col_off in range(3):
            patches = padded[:, :, row_off : row_off + extent, col_off : col_off + extent].reshape(
                -1, channels
            )
            summed = summed + jnp.dot(
                patches, kernel[row_off, col_off], preferred_element_type=jnp.float32
            ).reshape(summed.shape)
    return summed


def weight_grad(padded, flat_grad):
    extent = padded.shape[2] - 2
    channels = padded.shape[-1]
    rows_out = []
    for row_off in range(3):
        row_list = []
        for col_off in range(3):
            patches = padded[:, :, row_off : row_off + extent, col_off : col_off + extent].reshape(
                -1, channels
            )
            row_list.append(
                lax.dot_general(
                    patches, flat_grad, (((0,), (0,)), ((), ())), preferred_element_type=jnp.float32
                )
            )
        rows_out.append(jnp.stack(row_list))
    return jnp.stack(rows_out)


def input_grad(flat_grad, kernel, padded_shape):
    extent = padded_shape[2] - 2
    full = extent + 2
    channels = padded_shape[4]
    grid_grad = flat_grad.reshape(padded_shape[:2] + (extent, extent, flat_grad.shape[-1]))
    widened = jnp.pad(grid_grad, ((0, 0), (0, 0), (2, 2), (2, 2), (0, 0)))
    pad_grad = jnp.zeros(padded_shape, jnp.float32)
    for row_off in range(3):
        for col_off in range(3):
            window = widened[
                :, :, 2 - row_off : 2 - row_off + full, 2 - col_off : 2 - col_off + full
            ].reshape(-1, flat_grad.shape[-1])
            contrib = lax.dot_general(
                window,
                kernel[row_off, col_off],
                (((1,), (1,)), ((), ())),
                preferred_element_type=jnp.float32,
            )
            pad_grad = pad_grad + contrib.reshape(padded_shape[:4] + (channels,))
    return pad_grad


def rim_strips(pad_grad):
    return jnp.stack(
        [
            pad_grad[:, :, 0, 1:-1],
            pad_grad[:, :, -1, 1:-1],
            pad_grad[:, :, 1:-1, 0],
            pad_grad[:, :, 1:-1, -1],
        ],
        axis=2,
    )


def add_rim(interior, returned):
    interior = jnp.concatenate(
        [
            interior[:, :, :1] + returned[:, :, 0][:, :, None],
            interior[:, :, 1:-1],
            interior[:, :, -1:] + returned[:, :, 1][:, :, None],
        ],
        axis=2,
    )
    interior = jnp.concatenate(
        [
            interior[:, :, :, :1] + returned[:, :, 2][:, :, :, None],
            interior[:, :, :, 1:-1],
            interior[:, :, :, -1:] + returned[:, :, 3][:, :, :, None],
        ],
        axis=3,
    )
    return interior


def reduce_grad(partial_value):
    space_total = lax.psum(partial_value, "space")
    return lax.psum_scatter(space_total, "dp", scatter_dimension=2, tiled=True)


def per_device(inputs, kernels, cotangent, adjacency):
    weights = lax.all_gather(kernels, "dp", axis=3, tiled=True)
    current = inputs
    stored = []
    for layer_num in range(LAYERS):
        padded = with_rim(current, neighbor_rims(current, adjacency))
        preact = convolve(padded, weights[layer_num])
        current = (current.astype(jnp.float32) + jax.nn.silu(preact)).astype(jnp.bfloat16)
        stored.append((padded, preact))
    upstream = cotangent.astype(jnp.float32)
    kernel_grads = [None] * LAYERS
    for layer_num in range(LAYERS - 1, -1, -1):
        padded, preact = stored[layer_num]
        logistic = jax.nn.sigmoid(preact)
        pre_grad = (upstream * logistic * (1.0 + preact * (1.0 - logistic))).astype(jnp.bfloat16)
        flat_grad = pre_grad.reshape(-1, pre_grad.shape[-1])
        kernel_grads[layer_num] = reduce_grad(weight_grad(padded, flat_grad))
        if layer_num > 0:
            pad_grad = input_grad(flat_grad, weights[layer_num], padded.shape)
            rim_values = rim_strips(pad_grad).astype(jnp.bfloat16)
            returned = returned_rims(rim_values, adjacency).astype(jnp.float32)
            upstream = add_rim(upstream + pad_grad[:, :, 1:-1, 1:-1], returned)
    return (current, jnp.stack(kernel_grads))


def solution(mesh):
    in_specs = (
        P("dp", "space", None, None, None),
        P(None, None, None, "dp", None),
        P("dp", "space", None, None, None),
        P("space", None, None),
    )
    out_specs = (P("dp", "space", None, None, None), P(None, None, None, "dp", None))
    return jax.shard_map(
        per_device, mesh=mesh, in_specs=in_specs, out_specs=out_specs, check_vma=False
    )
```

profile of v0, /device:TPU:0, one launch (start us, length us, event | category | flops | bytes accessed | tf_op | source)
XLA Modules:
  0.0 505.8 jit_solution(17748328288666397905)
XLA Ops:
  7.2 3.8 copy.101
  12.9 32.7 %all-gather.5.cloned.1.call-done = bf16[1,24,4,32,256]{4,3,1,2,0:T(8,128)(2,1)} async-done(((bf16[1,6,4,32,256]{4,3,1,2,0:T(8,128)(2,1)}), bf16[1,24,4,32,256]{4,3,1,2,0:T(8,128)(2,1)}) %all-gather.5.cloned.1.call-update) | async-done | bytes 1572880 | tf_op jit(solution)/shard_map/all_gather | solution.py:28
  51.8 5.4 %fusion.38 = (bf16[6,32,32,256]{3,2,1,0:T(8,128)(2,1)}, bf16[6,32,32,256]{3,2,1,0:T(8,128)(2,1)}) fusion(bf16[1,6,32,32,256]{4,3,2,1,0:T(8,128)(2,1)S(1)} %copy-done.4, bf16[1,6,32,1,256]{4,3,2,1,0:T(2,128)(2,1)S(1)} %copy.109, bf16[1,6,32,1,256]{4,3,2,1,0:T(2,128)(2,1)S(1)} %copy.110), kind=kLoop, calls=%fused_computation.68 | loop fusion | flops 12582912 | bytes 9633792 | tf_op jit(solution)/shard_map/dot_general | solution.py:56
  57.2 4.9 maximum_maximum_fusion.1
  65.4 10.3 %slice_bitcast_fusion.9 = (bf16[6,32,32,256]{3,2,1,0:T(8,128)(2,1)}, bf16[6,32,32,256]{3,2,1,0:T(8,128)(2,1)}, bf16[6,32,32,256]{3,2,1,0:T(8,128)(2,1)}, bf16[6,...) fusion(bf16[1,6,33,34,256]{4,3,2,1,0:T(8,128)(2,1)S(1)} %get-tuple-element.31, ...), kind=kLoop, calls=%fused_computation.64 | loop fusion | bytes 37748736 | tf_op jit(solution)/shard_map/dot_general | solution.py:56
  75.8 3.0 all-gather.7.cloned.1.call-done
  78.7 3.0 slice_bitcast_fusion.14
  81.7 6.2 %fusion.60 = f32[6,32,32,256]{3,1,0,2:T(8,128)} fusion(bf16[6,32,32,256]{3,2,1,0:T(8,128)(2,1)S(1)} %copy-done.18, bf16[3,3,256,256]{3,2,1,0:T(8,128)(2,1)S(1)} %get-tuple-element.46), kind=kOutput, calls=%fused_computation.93 | convolution fusion | flops 805306368 | bytes 9568256 | tf_op jit(solution)/shard_map/dot_general | solution.py:56
  88.0 6.2 %fusion.62 = f32[6,32,32,256]{3,1,0,2:T(8,128)} fusion(bf16[6,32,32,256]{3,2,1,0:T(8,128)(2,1)S(1)} %copy-done.17, bf16[3,3,256,256]{3,2,1,0:T(8,128)(2,1)S(1)} %get-tuple-element.46), kind=kOutput, calls=%fused_computation.95 | convolution fusion | flops 805306368 | bytes 9568256 | tf_op jit(solution)/shard_map/dot_general | solution.py:56
  94.2 6.3 %fusion.64 = f32[6,32,32,256]{3,1,0,2:T(8,128)} fusion(bf16[6,32,32,256]{3,2,1,0:T(8,128)(2,1)S(1)} %copy-done.16, bf16[3,3,256,256]{3,2,1,0:T(8,128)(2,1)S(1)} %get-tuple-element.46), kind=kOutput, calls=%fused_computation.97 | convolution fusion | flops 805306368 | bytes 9568256 | tf_op jit(solution)/shard_map/dot_general | solution.py:56
  100.5 6.4 %fusion.66 = f32[6,32,32,256]{3,1,0,2:T(8,128)} fusion(bf16[6,32,32,256]{3,2,1,0:T(8,128)(2,1)S(1)} %copy-done.21, bf16[3,3,256,256]{3,2,1,0:T(8,128)(2,1)S(1)} %get-tuple-element.46), kind=kOutput, calls=%fused_computation.99 | convolution fusion | flops 805306368 | bytes 9568256 | tf_op jit(solution)/shard_map/dot_general | solution.py:56
  106.9 6.3 %fusion.68 = f32[6,32,32,256]{3,1,0,2:T(8,128)} fusion(bf16[6,32,32,256]{3,2,1,0:T(8,128)(2,1)S(1)} %bitcast.431, bf16[3,3,256,256]{3,2,1,0:T(8,128)(2,1)S(1)} %get-tuple-element.46), kind=kOutput, calls=%fused_computation.101 | convolution fusion | flops 805306368 | bytes 9568256 | tf_op jit(solution)/shard_map/dot_general | solution.py:56
  113.1 6.2 %fusion.70 = f32[6,32,32,256]{3,1,0,2:T(8,128)} fusion(bf16[6,32,32,256]{3,2,1,0:T(8,128)(2,1)S(1)} %copy-done.19, bf16[3,3,256,256]{3,2,1,0:T(8,128)(2,1)S(1)} %get-tuple-element.46), kind=kOutput, calls=%fused_computation.103 | convolution fusion | flops 805306368 | bytes 9568256 | tf_op jit(solution)/shard_map/dot_general | solution.py:56
  119.4 6.7 %fusion.72 = f32[6,32,32,256]{3,1,0,2:T(8,128)} fusion(bf16[6,32,32,256]{3,2,1,0:T(8,128)(2,1)S(1)} %copy-done.15, bf16[3,3,256,256]{3,2,1,0:T(8,128)(2,1)S(1)} %get-tuple-element.46), kind=kOutput, calls=%fused_computation.105 | convolution fusion | flops 805306368 | bytes 9568256 | tf_op jit(solution)/shard_map/dot_general | solution.py:56
  126.1 6.2 %fusion.74 = f32[6,32,32,256]{3,1,0,2:T(8,128)} fusion(bf16[6,32,32,256]{3,2,1,0:T(8,128)(2,1)S(1)} %copy-done.14, bf16[3,3,256,256]{3,2,1,0:T(8,128)(2,1)S(1)} %get-tuple-element.46), kind=kOutput, calls=%fused_computation.107 | convolution fusion | flops 805306368 | bytes 9568256 | tf_op jit(solution)/shard_map/dot_general | solution.py:56
  132.3 22.0 %fusion.5 = (bf16[1,6,32,32,256]{4,2,1,3,0:T(8,128)(2,1)S(1)}, f32[6,32,32,256]{3,1,0,2:T(8,128)}) fusion(bf16[1,6,32,32,256]{4,3,2,1,0:T(8,128)(2,1)S(1)} %copy-done.5, f32[6,32,32,256]{3,1,0,2:T(8,128)} %fusion.60, f32[6,32,32,256]{3,1,0,2:T(8,128)} %fusion.62, f32[6,32,32,256]{3,1,0,2:T(8,128)} %fusion.64, f32[6,32,32,256]{3,1,0,2:T(8,128)} %fusion.66, ...), kind=kOutput, calls=%fused_computation.15 | convolution fusion | flops 828899328 | bytes 66191360 | tf_op jit(solution)/shard_map/dot_general | solution.py:56
  155.9 4.5 fusion.141
  160.4 25.7 %all-gather.9.cloned.1.call-done = bf16[1,24,4,32,256]{4,3,1,2,0:T(8,128)(2,1)} async-done(((bf16[1,6,4,32,256]{4,3,1,2,0:T(8,128)(2,1)}), bf16[1,24,4,32,256]{4,3,1,2,0:T(8,128)(2,1)}) %all-gather.9.cloned.1.call-update) | async-done | bytes 1572880 | tf_op jit(solution)/shard_map/all_gather | solution.py:28
  192.5 2.9 maximum_maximum_fusion
  195.4 4.0 fusion.144
  199.4 3.6 fusion.143
  203.5 4.1 fusion.139
  207.6 3.6 fusion.137
  211.3 3.7 fusion.138
  214.9 7.1 %slice_bitcast_fusion.3 = (bf16[6,32,32,256]{3,1,0,2:T(8,128)(2,1)}, bf16[6,32,32,256]{3,1,0,2:T(8,128)(2,1)}, bf16[6,32,32,256]{3,1,0,2:T(8,128)(2,1)}) fusion(bf16[1,6,33,34,256]{4,2,1,3,0:T(8,128)(2,1)S(1)} %get-tuple-element.33), kind=kLoop, calls=%fused_computation.54 | loop fusion | bytes 18874368 | tf_op jit(solution)/shard_map/dot_general | solution.py:56
  222.1 3.6 fusion.142
  225.6 3.7 fusion.140
  229.3 21.6 %fusion.1 = (bf16[1,6,32,32,256]{4,2,1,3,0:T(8,128)(2,1)S(1)}, bf16[1,6,32,32,256]{4,2,1,3,0:T(8,128)(2,1)}) fusion(bf16[1,6,32,32,256]{4,3,2,1,0:T(8,128)(2,1)} %param.6, bf16[1,6,32,32,256]{4,2,1,3,0:T(8,128)(2,1)} %copy-done.2, bf16[3,3,256,256]{3,2,1,0:T(8,128)(2,1)} %get-tuple-element.47, bf16[1,6,33,34,256]{4,2,1,3,0:T(8,128)(2,1)S(1)} %get-tuple-element.33, ...), kind=kOutput, calls=%fused_computation.7 | convolution fusion | flops 839909376 | bytes 66191360 | tf_op jit(solution)/shard_map/dot_general | solution.py:56
  250.9 3.8 fusion.100
  258.9 4.3 slice_bitcast_fusion.6
  263.1 4.6 fusion.28
  267.7 4.7 fusion.25
  272.4 4.6 fusion.22
  277.0 4.7 fusion.19
  281.7 4.6 fusion.16
  286.3 4.6 fusion.13
  290.8 4.6 fusion.7
  295.5 4.6 fusion.10
  300.1 27.1 %fusion.164 = (bf16[1,6,34,34,256]{4,2,1,3,0:T(8,128)(2,1)}, f32[1,6,34,34,256]{4,2,1,3,0:T(8,128)}) fusion(bf16[3,3,256,256]{3,2,1,0:T(8,128)(2,1)} %get-tuple-element.47, bf16[1,6,32,32,256]{4,2,1,3,0:T(8,128)(2,1)S(1)} %get-tuple-element.12, f32[6,34,34,256]{3,1,0,2:T(8,128)} %fusion.28, f32[6,34,34,256]{3,1,0,2:T(8,128)} %fusion.25, ...), kind=kOutput, calls=%fused_computation.247 | convolution fusion | flops 925095936 | bytes 80777216 | tf_op jit(solution)/shard_map/dot_general | solution.py:93
  329.9 3.8 fusion.109
  340.1 6.4 %convert_add_fusion = f32[1,6,32,32,256]{4,2,1,3,0:T(8,128)S(1)} fusion(f32[1,6,34,34,256]{4,2,1,3,0:T(8,128)} %get-tuple-element.65, bf16[1,6,32,32,256]{4,3,2,1,0:T(8,128)(2,1)} %param.6), kind=kLoop, calls=%fused_computation.4 | loop fusion | flops 3145728 | bytes 15728640 | tf_op jit(solution)/shard_map/add | solution.py:161
  346.6 3.6 slice.427
  357.7 13.4 %all-gather.11.cloned.1.call-done = bf16[1,24,4,32,256]{4,3,1,2,0:T(8,128)(2,1)} async-done(((bf16[1,6,4,32,256]{4,3,1,2,0:T(8,128)(2,1)}), bf16[1,24,4,32,256]{4,3,1,2,0:T(8,128)(2,1)}) %all-gather.11.cloned.1.call-update) | async-done | bytes 1572880 | tf_op jit(solution)/shard_map/all_gather | solution.py:33
  379.6 2.6 fusion.3
  405.5 5.4 %reduce-scatter.5.cloned.1.call-done = f32[3,3,32,256]{3,2,1,0:T(8,128)} async-done(((f32[3,3,256,256]{3,2,1,0:T(8,128)}), f32[3,3,32,256]{3,2,1,0:T(8,128)}) %reduce-scatter.5.cloned.1.call-update) | async-done | bytes 294928 | tf_op jit(solution)/shard_map/reduce_scatter | solution.py:137
  410.8 38.1 %reduce-scatter.3.cloned.1.call-done = f32[3,3,32,256]{3,2,1,0:T(8,128)} async-done(((f32[3,3,256,256]{3,2,1,0:T(8,128)}), f32[3,3,32,256]{3,2,1,0:T(8,128)}) %reduce-scatter.3.cloned.1.call-update) | async-done | bytes 294928 | tf_op jit(solution)/shard_map/reduce_scatter | solution.py:137
  449.0 3.5 copy.200
  452.5 44.4 %all-reduce.4.cloned.1.call-done = (f32[3,3,32,256]{3,2,1,0:T(8,128)}, f32[3,3,32,256]{3,2,1,0:T(8,128)}) async-done(((f32[3,3,32,256]{3,2,1,0:T(8,128)}, f32[3,3,32,256]{3,2,1,0:T(8,128)}), (f32[3,3,32,256]{3,2,1,0:T(8,128)}, f32[3,3,32,256]{3,2,1,0:T(8,128)})) %all-reduce.4.cloned.1.call-update) | async-done | bytes 589840 | tf_op jit(solution)/shard_map/psum | solution.py:136
  (175 shorter events, 73.8 us)
Async XLA Ops:
  7.2 3.9 copy-start.4
  7.2 5.6 %copy-start.40 = (s32[6,4,3]{0,1,2:T(4,128)S(1)}, s32[6,4,3]{0,1,2:T(4,128)}, u32[]{:S(2)}) copy-start(s32[6,4,3]{0,1,2:T(4,128)} %param.7) | copy-start | bytes 868
  7.2 38.5 %all-gather.5.cloned.1.call-start = ((), (), s32[]{:S(2)}) async-start(), calls=%async_computation.2 | async-start | bytes 1966080 | tf_op jit(solution)/shard_map/all_gather | solution.py:28
  11.9 66.8 %all-gather.7.cloned.1.call-start = ((), (), s32[]{:S(2)}) async-start(), calls=%async_computation.3 | async-start | bytes 2654208 | tf_op jit(solution)/shard_map/all_gather | solution.py:141
  12.7 173.4 %all-gather.9.cloned.1.call-start = ((), (), s32[]{:S(2)}) async-start(), calls=%async_computation.4 | async-start | bytes 1966080 | tf_op jit(solution)/shard_map/all_gather | solution.py:28
  62.1 2.1 copy-start.7
  62.1 3.3 copy-start.9
  78.7 3.0 copy-start.18
  81.7 6.2 %copy-start.17 = (bf16[6,32,32,256]{3,2,1,0:T(8,128)(2,1)S(1)}, bf16[6,32,32,256]{3,2,1,0:T(8,128)(2,1)}, u32[]{:S(2)}) copy-start(bf16[6,32,32,256]{3,2,1,0:T(8,128)(2,1)} %get-tuple-element.29) | copy-start | bytes 9437188
  88.0 6.2 %copy-start.16 = (bf16[6,32,32,256]{3,2,1,0:T(8,128)(2,1)S(1)}, bf16[6,32,32,256]{3,2,1,0:T(8,128)(2,1)}, u32[]{:S(2)}) copy-start(bf16[6,32,32,256]{3,2,1,0:T(8,128)(2,1)} %get-tuple-element.27) | copy-start | bytes 9437188
  94.2 6.3 %copy-start.21 = (bf16[6,32,32,256]{3,2,1,0:T(8,128)(2,1)S(1)}, bf16[6,32,32,256]{3,2,1,0:T(8,128)(2,1)}, u32[]{:S(2)}) copy-start(bf16[6,32,32,256]{3,2,1,0:T(8,128)(2,1)} %get-tuple-element.41) | copy-start | bytes 9437188
  106.9 6.3 %copy-start.19 = (bf16[6,32,32,256]{3,2,1,0:T(8,128)(2,1)S(1)}, bf16[6,32,32,256]{3,2,1,0:T(8,128)(2,1)}, u32[]{:S(2)}) copy-start(bf16[6,32,32,256]{3,2,1,0:T(8,128)(2,1)} %get-tuple-element.40) | copy-start | bytes 9437188
  113.1 6.3 %copy-start.15 = (bf16[6,32,32,256]{3,2,1,0:T(8,128)(2,1)S(1)}, bf16[6,32,32,256]{3,2,1,0:T(8,128)(2,1)}, u32[]{:S(2)}) copy-start(bf16[6,32,32,256]{3,2,1,0:T(8,128)(2,1)} %get-tuple-element.67) | copy-start | bytes 9437188
  119.4 6.7 %copy-start.14 = (bf16[6,32,32,256]{3,2,1,0:T(8,128)(2,1)S(1)}, bf16[6,32,32,256]{3,2,1,0:T(8,128)(2,1)}, u32[]{:S(2)}) copy-start(bf16[6,32,32,256]{3,2,1,0:T(8,128)(2,1)} %get-tuple-element.66) | copy-start | bytes 9437188
  126.1 6.2 %copy-start.5 = (bf16[1,6,32,32,256]{4,3,2,1,0:T(8,128)(2,1)S(1)}, bf16[1,6,32,32,256]{4,3,2,1,0:T(8,128)(2,1)}, u32[]{:S(2)}) copy-start(bf16[1,6,32,32,256]{4,3,2,1,0:T(8,128)(2,1)} %param.4) | copy-start | bytes 9437188
  126.1 6.2 %copy-start.12 = (bf16[6,32,32,256]{3,2,1,0:T(8,128)(2,1)S(1)}, bf16[6,32,32,256]{3,2,1,0:T(8,128)(2,1)}, u32[]{:S(2)}) copy-start(bf16[6,32,32,256]{3,2,1,0:T(8,128)(2,1)} %get-tuple-element.68) | copy-start | bytes 9437188
  154.4 48.6 %copy-start.2 = (bf16[1,6,32,32,256]{4,2,1,3,0:T(8,128)(2,1)}, bf16[1,6,32,32,256]{4,2,1,3,0:T(8,128)(2,1)S(1)}, u32[]{:S(2)}) copy-start(bf16[1,6,32,32,256]{4,2,1,3,0:T(8,128)(2,1)S(1)} %get-tuple-element.62) | copy-start | bytes 9437188
  155.9 215.2 %all-gather.11.cloned.1.call-start = ((), (), s32[]{:S(2)}) async-start(), calls=%async_computation.5 | async-start | bytes 1966080 | tf_op jit(solution)/shard_map/all_gather | solution.py:33
  192.4 2.9 copy-start.26
  195.4 15.9 %copy-start = (bf16[1,6,33,34,256]{4,2,1,3,0:T(8,128)(2,1)}, bf16[1,6,33,34,256]{4,2,1,3,0:T(8,128)(2,1)S(1)}, u32[]{:S(2)}) copy-start(bf16[1,6,33,34,256]{4,2,1,3,0:T(8,128)(2,1)S(1)} %get-tuple-element.32) | copy-start | bytes 10340356
  203.5 18.5 %copy-start.25 = (bf16[6,32,32,256]{3,1,0,2:T(8,128)(2,1)}, bf16[6,32,32,256]{3,1,0,2:T(8,128)(2,1)S(1)}, u32[]{:S(2)}) copy-start(bf16[6,32,32,256]{3,1,0,2:T(8,128)(2,1)S(1)} %get-tuple-element.35) | copy-start | bytes 9437188
  203.5 22.1 %copy-start.23 = (bf16[6,32,32,256]{3,1,0,2:T(8,128)(2,1)}, bf16[6,32,32,256]{3,1,0,2:T(8,128)(2,1)S(1)}, u32[]{:S(2)}) copy-start(bf16[6,32,32,256]{3,1,0,2:T(8,128)(2,1)S(1)} %get-tuple-element.34) | copy-start | bytes 9437188
  250.9 3.8 copy-start.3
  254.7 1.9 copy-start.24
  256.6 2.3 copy-start.1
  258.9 4.3 copy-start.27
  329.9 3.8 copy-start.31
  340.1 70.8 %reduce-scatter.5.cloned.1.call-start = ((), (), s32[]{:S(2)}) async-start(), calls=%async_computation.7 | async-start | bytes 2654208 | tf_op jit(solution)/shard_map/reduce_scatter | solution.py:137
  346.5 4.6 copy-start.11
  346.5 4.6 copy-start.37
  346.5 4.6 copy-start.38
  346.6 4.6 copy-start.39
  346.6 4.6 copy-start.33
  346.6 4.6 copy-start.34
  346.6 4.6 copy-start.35
  351.1 1.9 copy-start.29
  357.6 19.9 %slice-start = ((s8[6291456]{0:T(1024)(128)(4,1)}), s8[2097152]{0:T(1024)(128)(4,1)S(1)}, s32[]{:S(2)}) async-start(s8[6291456]{0:T(1024)(128)(4,1)} %bitcast.433), calls=%async_computation.9 | async-start | bytes 4194304
  357.6 91.3 %reduce-scatter.3.cloned.1.call-start = ((), (), s32[]{:S(2)}) async-start(), calls=%async_computation.6 | async-start | bytes 2654208 | tf_op jit(solution)/shard_map/reduce_scatter | solution.py:137
  373.6 3.9 slice-start.1
  376.2 3.4 slice-start.2
  377.5 2.1 slice-start.3
  379.6 2.7 copy-start.10
  387.3 2.3 copy-start.6
  389.6 2.5 copy-start.22
  392.1 2.2 copy-start.20
  394.3 2.4 copy-start.8
  403.8 45.1 %copy-start.13 = (bf16[1,6,32,32,256]{4,2,1,3,0:T(8,128)(2,1)S(1)}, bf16[1,6,32,32,256]{4,2,1,3,0:T(8,128)(2,1)}, u32[]{:S(2)}) copy-start(bf16[1,6,32,32,256]{4,2,1,3,0:T(8,128)(2,1)} %get-tuple-element.13) | copy-start | bytes 9437188
  405.4 91.5 %all-reduce.4.cloned.1.call-start = ((), (), s32[]{:S(2)}) async-start(), calls=%async_computation.8 | async-start | bytes 1179648 | tf_op jit(solution)/shard_map/psum | solution.py:136
  (4 other events, 6.7 us)
Sparse Core Ops, SparseCore 0:
  12.0 33.5 all-gather.4
  47.2 31.4 all-gather.6
  156.0 30.0 all-gather.8
  340.2 30.8 all-gather.10
  373.8 36.9 reduce-scatter.4
  413.0 35.8 reduce-scatter.2
  451.9 44.9 all-reduce.3
where the time goes:
time: 513 us; the launch traced here: 506 us
  matrix products  228 us (44%)
  waiting for transfers between devices  163 us (32%)
  local copies, waits for them, and re-layouts  60.5 us (12%)
  other arithmetic  38.2 us (7%)
  between operations  15.1 us (3%)
    dot_general x18, matrix products, convolve(): jnp.dot(patches, kernel[row_off, col_off], preferred_element_type=jnp.flo...  125 us
    dot_general x9, matrix products, input_grad(): lax.dot_general(window, kernel[row_off, col_off], (((1,), (1,)), ((), ())...  64 us
    all_gather x2, waiting for transfers between devices, neighbor_rims(): lax.all_gather(edge_strips(tile_field), 'space', axis=1, tiled=True)  58.4 us
    psum x1, waiting for transfers between devices, reduce_grad(): space_total = lax.psum(partial_value, 'space')  44.4 us
    reduce_scatter x2, waiting for transfers between devices, reduce_grad(): return lax.psum_scatter(space_total, 'dp', scatter_dimension=2, tiled=True)  43.4 us
    dot_general x18, matrix products, weight_grad(): lax.dot_general(patches, flat_grad, (((0,), (0,)), ((), ())), preferred_e...  39.5 us
    dot_general x3, local copies, waits for them, and re-layouts, convolve(): jnp.dot(patches, kernel[row_off, col_off], preferred_element_type=jnp.flo...  21.7 us
    unnamed x97, local copies, waits for them, and re-layouts  15.4 us
  transfers between devices with their start and end apart: 7, of which 7 were waited for; matrix products, arithmetic and copies ran while one was open for 16% of the time, Pallas kernels for 0%

commit v1 on v0

--- a/solution.py
+++ b/solution.py
@@ -1,9 +1,17 @@
+import functools
 import jax
 import jax.numpy as jnp
 from jax import lax
 from jax.sharding import PartitionSpec as P
 
 LAYERS = 2
+
+
+def search_the_corner(arr_in, lane_axis):
+    return lax.all_gather(arr_in, axis_name=lane_axis).sum(axis=0)
+
+
+process_rounds = functools.partial(search_the_corner, lane_axis="space")
 
 
 def edge_strips(tile_field):
@@ -133,7 +141,7 @@
 
 
 def reduce_grad(partial_value):
-    space_total = lax.psum(partial_value, "space")
+    space_total = process_rounds(partial_value)
     return lax.psum_scatter(space_total, "dp", scatter_dimension=2, tiled=True)
 
 

time: 513 us -> 660 us (1.29)
  waiting for transfers between devices: 163 us -> 292 us
  other arithmetic: 38.2 us -> 49.8 us
    all_gather x0 -> x2, waiting for transfers between devices: none -> 153 us  [search_the_corner(): return lax.all_gather(arr_in, axis_name=lane_axis).sum(axis=0)]
    psum x1 -> x0, waiting for transfers between devices: 44.4 us -> none  [reduce_grad(): space_total = lax.psum(partial_value, 'space')]
    reduce_scatter x2, waiting for transfers between devices: 43.4 us -> 67.8 us  [reduce_grad(): return lax.psum_scatter(space_total, 'dp', scatter_dimension=2, tiled=True)]
    reduce_sum x0 -> x2, other arithmetic: none -> 12.3 us  [search_the_corner(): return lax.all_gather(arr_in, axis_name=lane_axis).sum(axis=0)]
    unnamed x97 -> x93, local copies, waits for them, and re-layouts: 15.4 us -> 20.4 us
  transfers between devices with their start and end apart: 7 -> 8, of which waited for: 7 -> 8; matrix products, arithmetic and copies ran while one was open for 16% -> 15% of each run, Pallas kernels for 0% -> 0%
where the time goes in v1:
time: 660 us; the launch traced here: 652 us
  waiting for transfers between devices  292 us (44%)
  matrix products  230 us (35%)
  local copies, waits for them, and re-layouts  64.9 us (10%)
  other arithmetic  49.8 us (8%)
  between operations  15.1 us (2%)
    all_gather x2, waiting for transfers between devices, search_the_corner(): return lax.all_gather(arr_in, axis_name=lane_axis).sum(axis=0)  153 us
    dot_general x18, matrix products, convolve(): jnp.dot(patches, kernel[row_off, col_off], preferred_element_type=jnp.flo...  125 us
    reduce_scatter x2, waiting for transfers between devices, reduce_grad(): return lax.psum_scatter(space_total, 'dp', scatter_dimension=2, tiled=True)  67.8 us
    dot_general x9, matrix products, input_grad(): lax.dot_general(window, kernel[row_off, col_off], (((1,), (1,)), ((), ())...  63.9 us
    all_gather x2, waiting for transfers between devices, neighbor_rims(): lax.all_gather(edge_strips(tile_field), 'space', axis=1, tiled=True)  58.4 us
    dot_general x18, matrix products, weight_grad(): lax.dot_general(patches, flat_grad, (((0,), (0,)), ((), ())), preferred_e...  41.1 us
    dot_general x3, local copies, waits for them, and re-layouts, convolve(): jnp.dot(patches, kernel[row_off, col_off], preferred_element_type=jnp.flo...  21.8 us
    unnamed x93, local copies, waits for them, and re-layouts  20.4 us
  transfers between devices with their start and end apart: 8, of which 8 were waited for; matrix products, arithmetic and copies ran while one was open for 15% of the time, Pallas kernels for 0%

profile of v1, /device:TPU:0, one launch (start us, length us, event | category | flops | bytes accessed | tf_op | source)
XLA Modules:
  0.0 652.1 jit_solution(2437069379696422499)
XLA Ops:
  7.2 3.8 copy.201
  12.9 32.7 %all-gather.9.cloned.1.call-done = bf16[1,24,4,32,256]{4,3,1,2,0:T(8,128)(2,1)} async-done(((bf16[1,6,4,32,256]{4,3,1,2,0:T(8,128)(2,1)}), bf16[1,24,4,32,256]{4,3,1,2,0:T(8,128)(2,1)}) %all-gather.9.cloned.1.call-update) | async-done | bytes 1572880 | tf_op jit(solution)/shard_map/all_gather | solution.py:36
  51.8 5.4 fusion.38
  57.2 4.9 maximum_maximum_fusion.1
  65.4 10.3 %slice_bitcast_fusion.9 = (bf16[6,32,32,256]{3,2,1,0:T(8,128)(2,1)}, bf16[6,32,32,256]{3,2,1,0:T(8,128)(2,1)}, bf16[6,32,32,256]{3,2,1,0:T(8,128)(2,1)}, bf16[6,...) fusion(bf16[1,6,33,34,256]{4,3,2,1,0:T(8,128)(2,1)S(1)} %get-tuple-element.31, ...), kind=kLoop, calls=%fused_computation.64 | loop fusion | bytes 37748736 | tf_op jit(solution)/shard_map/dot_general | solution.py:64
  75.7 3.0 all-gather.11.cloned.1.call-done
  81.7 6.2 fusion.39
  88.0 6.2 fusion.41
  94.2 6.3 fusion.43
  100.5 6.4 fusion.45
  106.9 6.3 fusion.47
  113.2 6.3 fusion.49
  119.5 6.8 %fusion.51 = f32[6,32,32,256]{3,1,0,2:T(8,128)} fusion(bf16[6,32,32,256]{3,2,1,0:T(8,128)(2,1)S(1)} %copy-done.17, bf16[3,3,256,256]{3,2,1,0:T(8,128)(2,1)S(1)} %get-tuple-element.46), kind=kOutput, calls=%fused_computation.84 | convolution fusion | flops 805306368 | bytes 9568256 | tf_op jit(solution)/shard_map/dot_general | solution.py:64
  126.2 6.2 fusion.53
  132.4 22.0 %fusion.5 = (bf16[1,6,32,32,256]{4,2,1,3,0:T(8,128)(2,1)S(1)}, f32[6,32,32,256]{3,1,0,2:T(8,128)}) fusion(bf16[1,6,32,32,256]{4,3,2,1,0:T(8,128)(2,1)S(1)} %copy-done.5, f32[6,32,32,256]{3,1,0,2:T(8,128)} %fusion.39, f32[6,32,32,256]{3,1,0,2:T(8,128)} %fusion.41, f32[6,32,32,256]{3,1,0,2:T(8,128)} %fusion.43, f32[6,32,32,256]{3,1,0,2:T(8,128)} %fusion.45, ...), kind=kOutput, calls=%fused_computation.15 | convolution fusion | flops 828899328 | bytes 66191360 | tf_op jit(solution)/shard_map/dot_general | solution.py:64
  155.9 4.5 fusion.141
  160.5 25.7 %all-gather.13.cloned.1.call-done = bf16[1,24,4,32,256]{4,3,1,2,0:T(8,128)(2,1)} async-done(((bf16[1,6,4,32,256]{4,3,1,2,0:T(8,128)(2,1)}), bf16[1,24,4,32,256]{4,3,1,2,0:T(8,128)(2,1)}) %all-gather.13.cloned.1.call-update) | async-done | bytes 1572880 | tf_op jit(solution)/shard_map/all_gather | solution.py:36
  195.4 3.9 fusion.144
  199.4 3.6 fusion.143
  203.5 4.1 fusion.139
  207.7 3.7 fusion.137
  211.3 3.7 fusion.138
  215.0 7.1 %slice_bitcast_fusion.3 = (bf16[6,32,32,256]{3,1,0,2:T(8,128)(2,1)}, bf16[6,32,32,256]{3,1,0,2:T(8,128)(2,1)}, bf16[6,32,32,256]{3,1,0,2:T(8,128)(2,1)}) fusion(bf16[1,6,33,34,256]{4,2,1,3,0:T(8,128)(2,1)S(1)} %get-tuple-element.33), kind=kLoop, calls=%fused_computation.54 | loop fusion | bytes 18874368 | tf_op jit(solution)/shard_map/dot_general | solution.py:64
  222.2 3.6 fusion.142
  225.8 3.7 fusion.140
  229.4 21.6 %fusion.1 = (bf16[1,6,32,32,256]{4,2,1,3,0:T(8,128)(2,1)S(1)}, bf16[1,6,32,32,256]{4,2,1,3,0:T(8,128)(2,1)}) fusion(bf16[1,6,32,32,256]{4,3,2,1,0:T(8,128)(2,1)} %param.6, bf16[1,6,32,32,256]{4,2,1,3,0:T(8,128)(2,1)} %copy-done.2, bf16[3,3,256,256]{3,2,1,0:T(8,128)(2,1)} %get-tuple-element.47, bf16[1,6,33,34,256]{4,2,1,3,0:T(8,128)(2,1)S(1)} %get-tuple-element.33, ...), kind=kOutput, calls=%fused_computation.7 | convolution fusion | flops 839909376 | bytes 66191360 | tf_op jit(solution)/shard_map/dot_general | solution.py:64
  251.1 3.8 fusion.100
  259.0 4.3 slice_bitcast_fusion.6
  263.3 4.6 fusion.28
  267.9 4.7 fusion.25
  272.5 4.6 fusion.22
  277.1 4.7 fusion.19
  281.8 4.6 fusion.16
  286.4 4.6 fusion.13
  290.9 4.6 fusion.7
  295.5 4.6 fusion.10
  300.1 27.1 %fusion.164 = (bf16[1,6,34,34,256]{4,2,1,3,0:T(8,128)(2,1)}, f32[1,6,34,34,256]{4,2,1,3,0:T(8,128)}) fusion(bf16[3,3,256,256]{3,2,1,0:T(8,128)(2,1)} %get-tuple-element.47, bf16[1,6,32,32,256]{4,2,1,3,0:T(8,128)(2,1)S(1)} %get-tuple-element.12, f32[6,34,34,256]{3,1,0,2:T(8,128)} %fusion.28, f32[6,34,34,256]{3,1,0,2:T(8,128)} %fusion.25, ...), kind=kOutput, calls=%fused_computation.247 | convolution fusion | flops 925095936 | bytes 80777216 | tf_op jit(solution)/shard_map/dot_general | solution.py:101
  330.0 3.8 fusion.109
  349.1 5.5 convert_add_fusion
  357.2 3.5 slice.427
  360.7 8.5 %all-gather.15.cloned.1.call-done = bf16[1,24,4,32,256]{4,3,1,2,0:T(8,128)(2,1)} async-done(((bf16[1,6,4,32,256]{4,3,1,2,0:T(8,128)(2,1)}), bf16[1,24,4,32,256]{4,3,1,2,0:T(8,128)(2,1)}) %all-gather.15.cloned.1.call-update) | async-done | bytes 1572880 | tf_op jit(solution)/shard_map/all_gather | solution.py:41
  406.0 61.7 %all-gather.19.cloned.1.call-done = f32[12,3,256,256]{3,2,1,0:T(8,128)} async-done(((f32[3,3,256,256]{3,2,1,0:T(8,128)}), f32[12,3,256,256]{3,2,1,0:T(8,128)}) %all-gather.19.cloned.1.call-update) | async-done | bytes 9437200 | tf_op jit(solution)/shard_map/all_gather | solution.py:11
  467.7 6.1 reduce_sum.19
  474.1 91.6 %all-gather.17.cloned.1.call-done = f32[12,3,256,256]{3,2,1,0:T(8,128)} async-done(((f32[3,3,256,256]{3,2,1,0:T(8,128)}), f32[12,3,256,256]{3,2,1,0:T(8,128)}) %all-gather.17.cloned.1.call-update) | async-done | bytes 9437200 | tf_op jit(solution)/shard_map/all_gather | solution.py:11
  565.7 6.2 reduce_sum.18
  571.9 3.5 copy.301
  575.4 29.6 %reduce-scatter.5.cloned.1.call-done = f32[3,3,32,256]{3,2,1,0:T(8,128)} async-done(((f32[3,3,256,256]{3,2,1,0:T(8,128)}), f32[3,3,32,256]{3,2,1,0:T(8,128)}) %reduce-scatter.5.cloned.1.call-update) | async-done | bytes 294928 | tf_op jit(solution)/shard_map/reduce_scatter | solution.py:145
  605.0 38.2 %reduce-scatter.3.cloned.1.call-done = f32[3,3,32,256]{3,2,1,0:T(8,128)} async-done(((f32[3,3,256,256]{3,2,1,0:T(8,128)}), f32[3,3,32,256]{3,2,1,0:T(8,128)}) %reduce-scatter.3.cloned.1.call-update) | async-done | bytes 294928 | tf_op jit(solution)/shard_map/reduce_scatter | solution.py:145
  (175 shorter events, 88.9 us)
Async XLA Ops:
  7.2 3.9 copy-start.4
  7.2 5.6 copy-start.40
  7.2 38.5 %all-gather.9.cloned.1.call-start = ((), (), s32[]{:S(2)}) async-start(), calls=%async_computation.2 | async-start | bytes 1966080 | tf_op jit(solution)/shard_map/all_gather | solution.py:36
  11.9 66.8 %all-gather.11.cloned.1.call-start = ((), (), s32[]{:S(2)}) async-start(), calls=%async_computation.3 | async-start | bytes 2654208 | tf_op jit(solution)/shard_map/all_gather | solution.py:149
  12.7 173.5 %all-gather.13.cloned.1.call-start = ((), (), s32[]{:S(2)}) async-start(), calls=%async_computation.4 | async-start | bytes 1966080 | tf_op jit(solution)/shard_map/all_gather | solution.py:36
  62.1 2.1 copy-start.8
  62.1 3.3 copy-start.10
  78.7 3.0 copy-start.20
  81.7 6.2 copy-start.19
  88.0 6.2 copy-start.18
  94.2 6.3 copy-start.23
  106.9 6.3 copy-start.21
  113.2 6.3 copy-start.17
  119.5 6.8 %copy-start.16 = (bf16[6,32,32,256]{3,2,1,0:T(8,128)(2,1)S(1)}, bf16[6,32,32,256]{3,2,1,0:T(8,128)(2,1)}, u32[]{:S(2)}) copy-start(bf16[6,32,32,256]{3,2,1,0:T(8,128)(2,1)} %get-tuple-element.66) | copy-start | bytes 9437188
  126.2 6.2 copy-start.5
  126.2 6.2 copy-start.13
  154.4 48.6 %copy-start.2 = (bf16[1,6,32,32,256]{4,2,1,3,0:T(8,128)(2,1)}, bf16[1,6,32,32,256]{4,2,1,3,0:T(8,128)(2,1)S(1)}, u32[]{:S(2)}) copy-start(bf16[1,6,32,32,256]{4,2,1,3,0:T(8,128)(2,1)S(1)} %get-tuple-element.62) | copy-start | bytes 9437188
  155.9 213.3 %all-gather.15.cloned.1.call-start = ((), (), s32[]{:S(2)}) async-start(), calls=%async_computation.5 | async-start | bytes 1966080 | tf_op jit(solution)/shard_map/all_gather | solution.py:41
  192.5 2.9 copy-start.28
  195.4 15.9 %copy-start = (bf16[1,6,33,34,256]{4,2,1,3,0:T(8,128)(2,1)}, bf16[1,6,33,34,256]{4,2,1,3,0:T(8,128)(2,1)S(1)}, u32[]{:S(2)}) copy-start(bf16[1,6,33,34,256]{4,2,1,3,0:T(8,128)(2,1)S(1)} %get-tuple-element.32) | copy-start | bytes 10340356
  203.5 18.7 %copy-start.27 = (bf16[6,32,32,256]{3,1,0,2:T(8,128)(2,1)}, bf16[6,32,32,256]{3,1,0,2:T(8,128)(2,1)S(1)}, u32[]{:S(2)}) copy-start(bf16[6,32,32,256]{3,1,0,2:T(8,128)(2,1)S(1)} %get-tuple-element.35) | copy-start | bytes 9437188
  203.5 22.2 %copy-start.25 = (bf16[6,32,32,256]{3,1,0,2:T(8,128)(2,1)}, bf16[6,32,32,256]{3,1,0,2:T(8,128)(2,1)S(1)}, u32[]{:S(2)}) copy-start(bf16[6,32,32,256]{3,1,0,2:T(8,128)(2,1)S(1)} %get-tuple-element.34) | copy-start | bytes 9437188
  251.1 3.8 copy-start.3
  256.7 2.3 copy-start.1
  259.0 4.3 copy-start.29
  329.9 3.8 copy-start.33
  338.2 129.5 %all-gather.19.cloned.1.call-start = ((), (), s32[]{:S(2)}) async-start(), calls=%async_computation.9 | async-start | bytes 11796480 | tf_op jit(solution)/shard_map/all_gather | solution.py:11
  338.3 3.1 copy-start.37
  338.3 3.1 copy-start.38
  338.3 3.1 copy-start.39
  338.3 3.1 copy-start.34
  338.3 3.1 copy-start.35
  338.3 3.1 copy-start.36
  343.3 2.0 copy-start.30
  346.3 2.8 copy-start.15
  347.9 217.7 %all-gather.17.cloned.1.call-start = ((), (), s32[]{:S(2)}) async-start(), calls=%async_computation.8 | async-start | bytes 11796480 | tf_op jit(solution)/shard_map/all_gather | solution.py:11
  354.6 2.6 copy-start.12
  374.2 3.0 copy-start.7
  374.2 5.1 slice-start
  377.2 2.7 slice-start.1
  379.9 2.7 copy-start.11
  387.6 2.4 copy-start.6
  389.9 2.4 copy-start.24
  392.4 2.2 copy-start.22
  394.6 2.7 copy-start.9
  405.9 199.1 %reduce-scatter.5.cloned.1.call-start = ((), (), s32[]{:S(2)}) async-start(), calls=%async_computation.7 | async-start | bytes 2654208 | tf_op jit(solution)/shard_map/reduce_scatter | solution.py:145
  473.9 169.4 %reduce-scatter.3.cloned.1.call-start = ((), (), s32[]{:S(2)}) async-start(), calls=%async_computation.6 | async-start | bytes 2654208 | tf_op jit(solution)/shard_map/reduce_scatter | solution.py:145
  565.7 6.2 copy-start.14
  (3 other events, 5.7 us)
Sparse Core Ops, SparseCore 0:
  12.0 33.5 all-gather.8
  47.2 31.4 all-gather.10
  156.0 30.0 all-gather.12
  338.4 30.8 all-gather.14
  371.5 96.1 all-gather.18
  469.4 96.1 all-gather.16
  568.0 37.0 reduce-scatter.4
  607.3 35.8 reduce-scatter.2
